TPU v7x, 128 devices: a whole 4x4x4 slice. The times are simulated.
128 devices in a mesh: grp: 2 (over y_lo), dev: 64 (over y_hi, x, z, core).
Axes of the slice: x: 4, y: 4 (y_hi: 2, y_lo: 2; y = y_hi * 2 + y_lo), z: 4, core: 2. Of those that a mesh axis runs over, the one named last changes fastest.
Arguments:
- weights: float32 [2, 64, 524288], P(None, None, ('grp', 'dev')), may hold values from -3 to 3
- owner_map: int32 [16], replicated, may hold values from 0 to 15, each once
- node_index: int32 [2, 64], replicated, may hold values from 0 to 7, as said below
Outputs:
- transformed: float32 [2, 64, 524288], P(None, None, ('grp', 'dev'))
Inputs may be any that keep to these rules, and one draw needn't show every extreme that they name: owner_map[col] = 2 k + rx puts coarse frequency column col at column slot rx of device group k, in grp+dev order, after the middle level; every value appears once. The 64 columns (node_index[0, t], node_index[1, t]) are distinct, so every pair of Chebyshev point numbers appears once.
All inputs are finite; a program needn't handle non-finite values.
Results may differ from a plain program's by a relative error of at most 0.0003.
Values sent between devices are 32-bit elements; how exact they have to be, the bound alone decides.
A program may use at most 128 MiB of HBM per device.

v0:
```python
import math
import jax
import jax.numpy as jnp
from jax import lax
from jax.sharding import PartitionSpec as P

NFREQ = 4096
CHEB = 8
TWO_PI = 2.0 * math.pi
HIGHEST = lax.Precision.HIGHEST


def from_partner(array, axis, bit):
    return lax.ppermute(array, axis, [(i, i ^ 1 << bit) for i in range(lax.axis_size(axis))])


def cheb_points():
    counter = jnp.arange(CHEB, dtype=jnp.float32)
    return 0.5 * jnp.cos(math.pi * (2.0 * counter + 1.0) / (2.0 * CHEB))


def node_select(node_index):
    numbers = jnp.arange(CHEB, dtype=jnp.int32)[None, :]
    select_x = (node_index[0][:, None] == numbers).astype(jnp.float32)
    select_y = (node_index[1][:, None] == numbers).astype(jnp.float32)
    return (select_x, select_y)


def node_offsets(node_index):
    points = cheb_points()
    select_x, select_y = node_select(node_index)
    return (
        jnp.sum(select_x * points[None, :], axis=1),
        jnp.sum(select_y * points[None, :], axis=1),
    )


def lagrange(places):
    points = cheb_points()
    rows_out = []
    for first_id in range(CHEB):
        product = jnp.ones_like(places)
        for other_id in range(CHEB):
            if other_id != first_id:
                product = (
                    product * (places - points[other_id]) / (points[first_id] - points[other_id])
                )
        rows_out.append(product)
    return jnp.stack(rows_out)


def child_tables(node_index):
    select_x, select_y = node_select(node_index)
    offset_x, offset_y = node_offsets(node_index)
    tables = []
    for child_id in range(4):
        basis_x = lagrange(0.5 * offset_x + 0.5 * (child_id % 2) - 0.25)
        basis_y = lagrange(0.5 * offset_y + 0.5 * (child_id // 2) - 0.25)
        table_x = jnp.sum(select_x[:, :, None] * basis_x[None, :, :], axis=1)
        table_y = jnp.sum(select_y[:, :, None] * basis_y[None, :, :], axis=1)
        tables.append(table_x * table_y)
    return jnp.stack(tables)


def speeds(place_x, place_y):
    speed_one = (2.0 + jnp.sin(TWO_PI * place_x) * jnp.sin(TWO_PI * place_y)) / 16.0
    speed_two = (2.0 + jnp.cos(TWO_PI * place_x) * jnp.cos(TWO_PI * place_y)) / 16.0
    return (speed_one * speed_one, speed_two * speed_two)


def radius(speed_x, speed_y, freq_x, freq_y):
    return jnp.sqrt(speed_x * freq_x * freq_x + speed_y * freq_y * freq_y + 1.0)


def freq_phase(place_x, place_y, freq_x, freq_y, centre_x, centre_y):
    speed_x, speed_y = speeds(place_x, place_y)
    numer_part = speed_x * (freq_x - centre_x) * (freq_x + centre_x) + speed_y * (
        freq_y - centre_y
    ) * (freq_y + centre_y)
    denom_part = radius(speed_x, speed_y, freq_x, freq_y) + radius(
        speed_x, speed_y, centre_x, centre_y
    )
    return TWO_PI * (
        place_x * (freq_x - centre_x) + place_y * (freq_y - centre_y) + numer_part / denom_part
    )


def space_phase(place_x, place_y, anchor_x, anchor_y, freq_x, freq_y):
    speed_x, speed_y = speeds(place_x, place_y)
    base_x, base_y = speeds(anchor_x, anchor_y)
    numer_part = (speed_x - base_x) * freq_x * freq_x + (speed_y - base_y) * freq_y * freq_y
    denom_part = radius(speed_x, speed_y, freq_x, freq_y) + radius(base_x, base_y, freq_x, freq_y)
    return TWO_PI * (
        (place_x - anchor_x) * freq_x + (place_y - anchor_y) * freq_y + numer_part / denom_part
    )


def rotate(values, phase_angle):
    cosine = jnp.cos(phase_angle)
    sine_part = jnp.sin(phase_angle)
    return jnp.stack(
        [values[0] * cosine - values[1] * sine_part, values[0] * sine_part + values[1] * cosine]
    )


def freq_level(pieces, space_x, space_y, box_x, box_y, level_id, offset_x, offset_y):
    width_a = 2.0 ** (-level_id)
    width_b = 2.0**level_id
    half_span = 0.5 * NFREQ
    centre_ax = ((space_x + 0.5) * width_a)[None, :]
    centre_ay = ((space_y + 0.5) * width_a)[None, :]
    centre_bx = ((box_x + 0.5) * width_b - half_span)[None, :]
    centre_by = ((box_y + 0.5) * width_b - half_span)[None, :]
    running = None
    for values, child_x, child_y, table_now in pieces:
        kid_x = ((2.0 * box_x + child_x + 0.5) * (0.5 * width_b) - half_span)[
            None, :
        ] + 0.5 * width_b * offset_x[:, None]
        kid_y = ((2.0 * box_y + child_y + 0.5) * (0.5 * width_b) - half_span)[
            None, :
        ] + 0.5 * width_b * offset_y[:, None]
        phase_angle = freq_phase(centre_ax, centre_ay, kid_x, kid_y, centre_bx, centre_by)
        product_term = jnp.einsum(
            "ts,rsn->rtn", table_now, rotate(values, -phase_angle), precision=HIGHEST
        )
        running = product_term if running is None else running + product_term
    node_x = centre_bx + width_b * offset_x[:, None]
    node_y = centre_by + width_b * offset_y[:, None]
    return rotate(running, freq_phase(centre_ax, centre_ay, node_x, node_y, centre_bx, centre_by))


def space_in(values, offset_x, offset_y, parent_x, parent_y, box_x, box_y, level_id):
    width_p = 2.0 ** (1 - level_id)
    anchor_x = ((parent_x + 0.5) * width_p)[None, :]
    anchor_y = ((parent_y + 0.5) * width_p)[None, :]
    freq_x = ((box_x + 0.5) * 2.0**level_id - 0.5 * NFREQ)[None, :]
    freq_y = ((box_y + 0.5) * 2.0**level_id - 0.5 * NFREQ)[None, :]
    place_x = anchor_x + width_p * offset_x[:, None]
    place_y = anchor_y + width_p * offset_y[:, None]
    return rotate(values, -space_phase(place_x, place_y, anchor_x, anchor_y, freq_x, freq_y))


def space_out(
    turned_in,
    table_now,
    offset_x,
    offset_y,
    parent_x,
    parent_y,
    child_x,
    child_y,
    box_x,
    box_y,
    level_id,
):
    width_a = 2.0 ** (-level_id)
    mixed_state = jnp.einsum("st,rsn->rtn", table_now, turned_in, precision=HIGHEST)
    anchor_x = ((parent_x + 0.5) * 2.0 * width_a)[None, :]
    anchor_y = ((parent_y + 0.5) * 2.0 * width_a)[None, :]
    place_x = ((2.0 * parent_x + child_x + 0.5) * width_a)[None, :] + width_a * offset_x[:, None]
    place_y = ((2.0 * parent_y + child_y + 0.5) * width_a)[None, :] + width_a * offset_y[:, None]
    freq_x = ((box_x + 0.5) * 2.0**level_id - 0.5 * NFREQ)[None, :]
    freq_y = ((box_y + 0.5) * 2.0**level_id - 0.5 * NFREQ)[None, :]
    return rotate(mixed_state, space_phase(place_x, place_y, anchor_x, anchor_y, freq_x, freq_y))


def first_geometry(step_id, group_ids, low_digit, high_digit, loc_ids, across):
    column = loc_ids % across
    row_id = loc_ids // across
    if step_id == 0:
        space_x = 2 * group_ids + low_digit % 2
        space_y = low_digit // 2
        box_x = 2 * column + high_digit % 2
        box_y = 2 * row_id + high_digit // 2
    else:
        space_x = 4 * group_ids + 2 * (low_digit % 2) + high_digit % 2
        space_y = 2 * (low_digit // 2) + high_digit // 2
        box_x = column
        box_y = row_id
    return [
        jnp.broadcast_to(jnp.asarray(entry_value), loc_ids.shape).astype(jnp.float32)
        for entry_value in (space_x, space_y, box_x, box_y)
    ]


def post_layout(loc_ids, per_source, rest_rows):
    source = loc_ids // per_source
    remain = loc_ids % per_source
    rest_x = remain // rest_rows
    rest_y = remain % rest_rows
    src_group = source // 16
    src_digits = source % 16
    low_digit = src_digits % 4
    high_digit = src_digits // 4
    middle_x = 4 * src_group + 2 * (low_digit % 2) + high_digit % 2
    middle_y = 2 * (low_digit // 2) + high_digit // 2
    return (middle_x, middle_y, rest_x, rest_y)


def second_geometry(step_id, middle_x, middle_y, column, rest_y, other_digit):
    if step_id == 0:
        parent_x = middle_x
        parent_y = middle_y
        box_x = 2 * column + other_digit % 2
        box_y = 2 * rest_y + other_digit // 2
    else:
        parent_x = 2 * middle_x + other_digit % 2
        parent_y = 2 * middle_y + other_digit // 2
        box_x = column
        box_y = rest_y
    return [
        jnp.asarray(entry_value).astype(jnp.float32)
        for entry_value in (parent_x, parent_y, box_x, box_y)
    ]


def owner_inverse(owner_map, count):
    counter = jnp.arange(count, dtype=jnp.int32)
    return jnp.sum(jnp.where(owner_map[None, :] == counter[:, None], counter[None, :], 0), axis=1)


def finish_levels(pair_state, owner_map, tables, offset_x, offset_y, first_level, across):
    node_count = pair_state.shape[1]
    per_dev = pair_state.shape[2]
    dev_count = lax.axis_size("dev")
    grp_count = lax.axis_size("grp")
    devices = dev_count * grp_count
    groups = devices // 16
    per_source = per_dev // devices
    rest_rows = per_dev // across // 4
    group_width = across // 4 // groups
    grp_index = lax.axis_index("grp")
    dev_index = lax.axis_index("dev")
    flat_index = grp_index * dev_count + dev_index
    own_group = flat_index // 16
    own_digits = flat_index % 16
    loc_index = jnp.arange(per_dev, dtype=jnp.int32)
    inverse = owner_inverse(owner_map, 16)
    blocks = pair_state.reshape(2, node_count, rest_rows, 2, 2, 16, 2, 2)
    blocks = jnp.transpose(blocks, (0, 1, 5, 3, 6, 4, 7, 2))
    blocks = jnp.take(blocks, inverse, axis=2)
    blocks = blocks.reshape(2, node_count, groups, group_width, 2, 2, 2, 2, rest_rows)
    blocks = jnp.transpose(blocks, (0, 1, 2, 4, 5, 6, 7, 3, 8))
    pair_state = lax.all_to_all(
        blocks.reshape(2, node_count, devices, per_source),
        ("grp", "dev"),
        split_axis=2,
        concat_axis=2,
        tiled=True,
    ).reshape(2, node_count, per_dev)
    middle_x, middle_y, rest_x, rest_y = post_layout(loc_index, per_source, rest_rows)
    column = jnp.take(inverse, own_group * group_width + rest_x)
    for step_id in range(2):
        if step_id == 0:
            own_digit = own_digits % 4
            other_digit = own_digits // 4
        else:
            own_digit = own_digits // 4
            other_digit = own_digits % 4
        level_id = first_level + 3 + step_id
        geometry = second_geometry(step_id, middle_x, middle_y, column, rest_y, other_digit)
        pair_sum = pair_state + from_partner(pair_state, "dev", 2 * step_id)
        summed = pair_sum + from_partner(pair_sum, "dev", 2 * step_id + 1)
        turned_in = space_in(
            summed, offset_x, offset_y, geometry[0], geometry[1], geometry[2], geometry[3], level_id
        )
        table_own = lax.dynamic_index_in_dim(tables, own_digit, 0, keepdims=False)
        pair_state = space_out(
            turned_in,
            table_own,
            offset_x,
            offset_y,
            geometry[0],
            geometry[1],
            (own_digit % 2).astype(jnp.float32),
            (own_digit // 2).astype(jnp.float32),
            geometry[2],
            geometry[3],
            level_id,
        )
    return pair_state


def body(weights, owner_map, node_index):
    per_dev = weights.shape[2]
    dev_count = lax.axis_size("dev")
    levels = NFREQ.bit_length() - 1
    first_level = levels // 2 - 2
    across = 2 ** (levels // 2)
    offset_x, offset_y = node_offsets(node_index)
    tables = child_tables(node_index)
    grp_index = lax.axis_index("grp")
    dev_index = lax.axis_index("dev")
    flat_index = grp_index * dev_count + dev_index
    own_group = flat_index // 16
    own_digits = flat_index % 16
    loc_index = jnp.arange(per_dev, dtype=jnp.int32)
    pair_state = weights
    for step_id in range(2):
        if step_id == 0:
            own_digit = own_digits % 4
            low_digit = own_digit
            high_digit = own_digits // 4
        else:
            own_digit = own_digits // 4
            low_digit = own_digits % 4
            high_digit = own_digit
        near_state = from_partner(pair_state, "dev", 2 * step_id)
        far_one, far_two = from_partner((pair_state, near_state), "dev", 2 * step_id + 1)
        arrived = [pair_state, near_state, far_one, far_two]
        pieces = []
        for delta_id in range(4):
            child_id = jnp.bitwise_xor(own_digit, delta_id)
            pieces.append(
                (
                    arrived[delta_id],
                    (child_id % 2).astype(jnp.float32),
                    (child_id // 2).astype(jnp.float32),
                    lax.dynamic_index_in_dim(tables, child_id, 0, keepdims=False),
                )
            )
        geometry = first_geometry(step_id, own_group, low_digit, high_digit, loc_index, across)
        pair_state = freq_level(
            pieces,
            geometry[0],
            geometry[1],
            geometry[2],
            geometry[3],
            first_level + 1 + step_id,
            offset_x,
            offset_y,
        )
    pair_state = finish_levels(
        pair_state, owner_map, tables, offset_x, offset_y, first_level, across
    )
    return pair_state


def solution(mesh):
    in_specs = (P(None, None, ("grp", "dev")), P(), P())
    out_specs = P(None, None, ("grp", "dev"))
    return jax.shard_map(body, mesh=mesh, in_specs=in_specs, out_specs=out_specs, check_vma=False)
```

profile of v0, /device:TPU:0, one launch (start us, length us, event | category | flops | bytes accessed | tf_op | source)
XLA Modules:
  0.0 573.0 jit_solution(9209224539109127543)
XLA Ops:
  83.6 6.3 %multiply_subtract_fusion.13 = (f32[1,64,4096]{2,1,0:T(8,128)S(1)}, f32[1,64,4096]{2,1,0:T(8,128)S(1)}) fusion(f32[2,64,4096]{2,1,0:T(8,128)} %param.3, f32[4096]{0:T(1024)S(1)} %get-tuple-element.154, f32[]{:T(128)S(6)} %mul.7297, f32[]{:T(128)S(6)} %mul.7291, f32[4096]{0:T(1024)S(1)} %fusion.362, f32[64]{0:T(128)S(1)} %get-tuple-element.115, ...), kind=kLoop, calls=%fused_computation.399 | loop fusion | flops 8126464 | bytes 4276752 | tf_op jit(solution)/shard_map/sub | solution.py:102
  92.5 5.1 multiply_subtract_fusion.12
  99.6 6.8 %multiply_subtract_fusion.11 = (f32[1,64,4096]{2,1,0:T(8,128)S(1)}, f32[1,64,4096]{2,1,0:T(8,128)S(1)}) fusion(f32[2,64,4096]{2,1,0:T(8,128)} %collective-permute-done.1, f32[4096]{0:T(1024)S(1)} %get-tuple-element.154, f32[]{:T(128)S(6)} %mul.7297, f32[]{:T(128)S(6)} %mul.7291, f32[4096]{0:T(1024)S(1)} %fusion.362, f32[64]{0:T(128)S(1)} %get-tuple-element.115, ...), kind=kLoop, calls=%fused_computation.395 | loop fusion | flops 8126464 | bytes 4276752 | tf_op jit(solution)/shard_map/sub | solution.py:102
  108.5 31.6 %collective-permute-done.2 = f32[2,64,4096]{2,1,0:T(8,128)S(1)} collective-permute-done((f32[2,64,4096]{2,1,0:T(8,128)S(1)}, f32[2,64,4096]{2,1,0:T(8,128)S(1)}, u32[]{:S(2)}, u32[]{:S(2)}) %collective-permute-start.2) | collective-permute-done | bytes 2097184 | tf_op jit(solution)/shard_map/ppermute | solution.py:14
  140.2 5.1 multiply_subtract_fusion.10
  147.3 10.1 %multiply_subtract_fusion.8 = (f32[1,64,4096]{2,1,0:T(8,128)S(1)}, f32[1,64,4096]{2,1,0:T(8,128)S(1)}, f32[1,64,4096]{2,1,0:T(8,128)S(1)}) fusion(f32[4096]{0:T(1024)S(1)} %get-tuple-element.195, f32[]{:T(128)S(6)} %mul.7617, f32[]{:T(128)S(6)} %mul.7611, f32[4096]{0:T(1024)S(1)} %get-tuple-element.194, f32[64]{0:T(128)S(1)} %get-tuple-element.114, ...), kind=kLoop, calls=%fused_computation.389 | loop fusion | flops 15204352 | bytes 5374496 | tf_op jit(solution)/shard_map/sub | solution.py:102
  164.2 43.7 %collective-permute-done.3 = f32[2,64,4096]{2,1,0:T(8,128)} collective-permute-done((f32[2,64,4096]{2,1,0:T(8,128)}, f32[2,64,4096]{2,1,0:T(8,128)}, u32[]{:S(2)}, u32[]{:S(2)}) %collective-permute-start.3) | collective-permute-done | bytes 2097184 | tf_op jit(solution)/shard_map/ppermute | solution.py:14
  209.5 6.3 %multiply_subtract_fusion.7 = (f32[1,64,4096]{2,1,0:T(8,128)S(1)}, f32[1,64,4096]{2,1,0:T(8,128)S(1)}) fusion(f32[2,64,4096]{2,1,0:T(8,128)} %collective-permute-done.3, f32[4096]{0:T(1024)S(1)} %get-tuple-element.195, f32[]{:T(128)S(6)} %mul.7617, f32[]{:T(128)S(6)} %mul.7611, f32[4096]{0:T(1024)S(1)} %get-tuple-element.194, f32[64]{0:T(128)S(1)} %get-tuple-element.114, ...), kind=kLoop, calls=%fused_computation.387 | loop fusion | flops 8126464 | bytes 4276752 | tf_op jit(solution)/shard_map/sub | solution.py:102
  215.8 6.3 %multiply_subtract_fusion.6 = (f32[1,64,4096]{2,1,0:T(8,128)S(1)}, f32[1,64,4096]{2,1,0:T(8,128)S(1)}) fusion(f32[2,64,4096]{2,1,0:T(8,128)} %collective-permute-done.4, f32[4096]{0:T(1024)S(1)} %get-tuple-element.195, f32[]{:T(128)S(6)} %mul.7617, f32[]{:T(128)S(6)} %mul.7611, f32[4096]{0:T(1024)S(1)} %get-tuple-element.194, f32[64]{0:T(128)S(1)} %get-tuple-element.114, ...), kind=kLoop, calls=%fused_computation.385 | loop fusion | flops 8126464 | bytes 4276752 | tf_op jit(solution)/shard_map/sub | solution.py:102
  222.1 32.4 %collective-permute-done.5 = f32[2,64,4096]{2,1,0:T(8,128)} collective-permute-done((f32[2,64,4096]{2,1,0:T(8,128)}, f32[2,64,4096]{2,1,0:T(8,128)}, u32[]{:S(2)}, u32[]{:S(2)}) %collective-permute-start.5) | collective-permute-done | bytes 2097184 | tf_op jit(solution)/shard_map/ppermute | solution.py:14
  254.6 11.4 %multiply_subtract_fusion.5 = (f32[1,64,4096]{2,1,0:T(8,128)S(1)}, f32[1,64,4096]{2,1,0:T(8,128)S(1)}, f32[1,64,4096]{2,1,0:T(8,128)S(1)}) fusion(f32[2,64,4096]{2,1,0:T(8,128)} %collective-permute-done.5, f32[4096]{0:T(1024)S(1)} %get-tuple-element.195, f32[]{:T(128)S(6)} %mul.7617, f32[]{:T(128)S(6)} %mul.7611, f32[4096]{0:T(1024)S(1)} %get-tuple-element.194, ...), kind=kLoop, calls=%fused_computation.383 | loop fusion | flops 15466496 | bytes 7455248 | tf_op jit(solution)/shard_map/sub | solution.py:102
  274.2 6.4 %multiply_subtract_fusion.4 = (f32[1,64,4096]{2,1,0:T(8,128)}, f32[1,64,4096]{2,1,0:T(8,128)S(1)}) fusion(f32[2,64,4096]{2,1,0:T(8,128)S(1)} %fusion, f32[4096]{0:T(1024)S(1)} %get-tuple-element.195, f32[]{:T(128)S(6)} %mul.7617, f32[]{:T(128)S(6)} %mul.7611, f32[64]{0:T(128)S(1)} %get-tuple-element.116, f32[4096]{0:T(1024)S(1)} %get-tuple-element.194, ...), kind=kLoop, calls=%fused_computation.381 | loop fusion | flops 7864320 | bytes 4243984 | tf_op jit(solution)/shard_map/sub | solution.py:102
  289.6 5.0 gather_fusion
  304.6 40.3 %all_to_all.5 = f32[128,1,4096]{2,1,0:T(1,128)} all-to-all(f32[128,1,4096]{2,1,0:T(1,128)S(1)} %reshape.12153), channel_id=1, replica_groups=mesh['grp'=2,'dev'=64] {'grp','dev'}, dimensions={0} | all-to-all | bytes 4194304 | tf_op jit(solution)/shard_map/all_to_all | solution.py:244
  345.4 7.3 %reduce.18 = f32[128,4096]{1,0:T(8,128)S(1)} reduce(f32[128,1,4096]{2,1,0:T(1,128)} %all_to_all.5, f32[]{:T(128)} %broadcast.18834), dimensions={1}, to_apply=%all_to_all.3.reduce_sub_computation | reduce | bytes 4194308 | tf_op jit(solution)/shard_map/all_to_all | solution.py:244
  355.7 4.7 copy.35
  375.2 5.7 multiply_add_fusion.16
  381.2 34.5 %collective-permute-done.7 = f32[2,64,4096]{2,1,0:T(8,128)S(1)} collective-permute-done((f32[2,64,4096]{2,1,0:T(8,128)S(1)}, f32[2,64,4096]{2,1,0:T(8,128)S(1)}, u32[]{:S(2)}, u32[]{:S(2)}) %collective-permute-start.7) | collective-permute-done | bytes 2097184 | tf_op jit(solution)/shard_map/ppermute | solution.py:14
  416.0 13.1 %multiply_subtract_fusion.3 = (f32[1,64,4096]{2,1,0:T(8,128)S(1)}, f32[1,64,4096]{2,1,0:T(8,128)S(1)}) fusion(f32[2,64,4096]{2,1,0:T(8,128)S(1)} %add.5384, f32[4096]{0:T(1024)S(1)} %get-tuple-element.13, f32[4096]{0:T(1024)S(1)} %get-tuple-element.203, f32[4096]{0:T(1024)S(1)} %get-tuple-element.204, f32[4096]{0:T(1024)S(1)} %get-tuple-element.158, ...), kind=kLoop, calls=%fused_computation.379 | loop fusion | flops 10747904 | bytes 4309504 | tf_op jit(solution)/shard_map/sub | solution.py:102
  431.1 12.9 %multiply_subtract_fusion.2 = (f32[1,64,4096]{2,1,0:T(8,128)S(1)}, f32[1,64,4096]{2,1,0:T(8,128)S(1)}) fusion(f32[2,64,4096]{2,1,0:T(8,128)S(1)} %convolution_bitcast_fusion.1, f32[4096]{0:T(1024)S(1)} %get-tuple-element.13, f32[4096]{0:T(1024)S(1)} %get-tuple-element.203, f32[4096]{0:T(1024)S(1)} %get-tuple-element.204, f32[4096]{0:T(1024)S(1)} %get-tuple-element.158, ...), kind=kLoop, calls=%fused_computation.377 | loop fusion | flops 10485760 | bytes 4342272 | tf_op jit(solution)/shard_map/sub | solution.py:102
  444.9 47.6 %collective-permute-done.8 = f32[2,64,4096]{2,1,0:T(8,128)S(1)} collective-permute-done((f32[2,64,4096]{2,1,0:T(8,128)S(1)}, f32[2,64,4096]{2,1,0:T(8,128)S(1)}, u32[]{:S(2)}, u32[]{:S(2)}) %collective-permute-start.8) | collective-permute-done | bytes 2097184 | tf_op jit(solution)/shard_map/ppermute | solution.py:14
  495.0 46.0 %collective-permute-done.9 = f32[2,64,4096]{2,1,0:T(8,128)} collective-permute-done((f32[2,64,4096]{2,1,0:T(8,128)}, f32[2,64,4096]{2,1,0:T(8,128)}, u32[]{:S(2)}, u32[]{:S(2)}) %collective-permute-start.9) | collective-permute-done | bytes 2097184 | tf_op jit(solution)/shard_map/ppermute | solution.py:14
  543.5 13.1 %multiply_subtract_fusion.1 = (f32[1,64,4096]{2,1,0:T(8,128)S(1)}, f32[1,64,4096]{2,1,0:T(8,128)S(1)}) fusion(f32[2,64,4096]{2,1,0:T(8,128)S(1)} %fusion.460, f32[4096]{0:T(1024)S(1)} %get-tuple-element.87, f32[4096]{0:T(1024)S(1)} %get-tuple-element.152, f32[4096]{0:T(1024)S(1)} %get-tuple-element.153, f32[4096]{0:T(1024)S(1)} %multiply_add_fusion.14, ...), kind=kLoop, calls=%fused_computation.375 | loop fusion | flops 10747904 | bytes 4309504 | tf_op jit(solution)/shard_map/sub | solution.py:102
  558.6 12.9 %multiply_subtract_fusion = (f32[2,64,4096]{2,1,0:T(8,128)S(1)}, f32[2,64,4096]{2,1,0:T(8,128)S(1)}) fusion(f32[2,64,4096]{2,1,0:T(8,128)S(1)} %convolution_bitcast_fusion, f32[4096]{0:T(1024)S(1)} %get-tuple-element.87, f32[4096]{0:T(1024)S(1)} %get-tuple-element.152, ...), kind=kLoop, output_to_operand_aliasing={{0}: (12, {}), {1}: (12, {})}, calls=%fused_computation.373 | loop fusion | flops 10485760 | bytes 4342784 | tf_op jit(solution)/shard_map/sub | solution.py:102
  (132 shorter events, 86.5 us)
Async XLA Ops:
  0.0 92.0 %collective-permute-start = (f32[2,64,4096]{2,1,0:T(8,128)}, f32[2,64,4096]{2,1,0:T(8,128)S(1)}, u32[]{:S(2)}, u32[]{:S(2)}) collective-permute-start(f32[2,64,4096]{2,1,0:T(8,128)} %param.3), channel_id=1, source_target_pairs={{0,1},{1,0},{2,3},{3,2},{4,5},{5,4},{6,7},{7,6},{8,9},{9,8},{10,11... | collective-permute-start | bytes 6291464 | tf_op jit(solution)/shard_map/ppermute | solution.py:14
  0.0 99.6 %collective-permute-start.1 = (f32[2,64,4096]{2,1,0:T(8,128)}, f32[2,64,4096]{2,1,0:T(8,128)}, u32[]{:S(2)}, u32[]{:S(2)}) collective-permute-start(f32[2,64,4096]{2,1,0:T(8,128)} %param.3), channel_id=1, source_target_pairs={{0,2},{1,3},{2,0},{3,1},{4,6},{5,7},{6,4},{7,5},{8,10},{9,11},{10,... | collective-permute-start | bytes 6291464 | tf_op jit(solution)/shard_map/ppermute | solution.py:14
  92.0 48.1 %collective-permute-start.2 = (f32[2,64,4096]{2,1,0:T(8,128)S(1)}, f32[2,64,4096]{2,1,0:T(8,128)S(1)}, u32[]{:S(2)}, u32[]{:S(2)}) collective-permute-start(f32[2,64,4096]{2,1,0:T(8,128)S(1)} %collective-permute-done), channel_id=1, source_target_pairs={{0,2},{1,3},{2,0},{3,1},{4,6},{5,7},{6,4},{7,5},{8,10},{9,11},{10,... | collective-permute-start | bytes 6291464 | tf_op jit(solution)/shard_map/ppermute | solution.py:14
  157.4 6.6 %copy-start.4 = (s32[16]{0:T(128)S(1)}, s32[16]{0:T(128)}, u32[]{:S(2)}) copy-start(s32[16]{0:T(128)} %param.4) | copy-start | bytes 196
  158.9 49.1 %collective-permute-start.3 = (f32[2,64,4096]{2,1,0:T(8,128)}, f32[2,64,4096]{2,1,0:T(8,128)}, u32[]{:S(2)}, u32[]{:S(2)}) collective-permute-start(f32[2,64,4096]{2,1,0:T(8,128)} %pad_maximum_fusion), channel_id=1, source_target_pairs={{0,4},{1,5},{2,6},{3,7},{4,0},{5,1},{6,2},{7,3},{8,12},{9,13},{10,... | collective-permute-start | bytes 6291464 | tf_op jit(solution)/shard_map/ppermute | solution.py:14
  162.5 53.3 %collective-permute-start.4 = (f32[2,64,4096]{2,1,0:T(8,128)}, f32[2,64,4096]{2,1,0:T(8,128)}, u32[]{:S(2)}, u32[]{:S(2)}) collective-permute-start(f32[2,64,4096]{2,1,0:T(8,128)} %pad_maximum_fusion), channel_id=1, source_target_pairs={{0,8},{1,9},{2,10},{3,11},{4,12},{5,13},{6,14},{7,15},{8,0},{9,1},... | collective-permute-start | bytes 6291464 | tf_op jit(solution)/shard_map/ppermute | solution.py:14
  207.9 46.6 %collective-permute-start.5 = (f32[2,64,4096]{2,1,0:T(8,128)}, f32[2,64,4096]{2,1,0:T(8,128)}, u32[]{:S(2)}, u32[]{:S(2)}) collective-permute-start(f32[2,64,4096]{2,1,0:T(8,128)} %collective-permute-done.3), channel_id=1, source_target_pairs={{0,8},{1,9},{2,10},{3,11},{4,12},{5,13},{6,14},{7,15},{8,0},{9,1},... | collective-permute-start | bytes 6291464 | tf_op jit(solution)/shard_map/ppermute | solution.py:14
  285.5 1.6 copy-start.1
  363.2 4.2 collective-permute-start.6
  367.8 48.0 %collective-permute-start.7 = (f32[2,64,4096]{2,1,0:T(8,128)S(1)}, f32[2,64,4096]{2,1,0:T(8,128)S(1)}, u32[]{:S(2)}, u32[]{:S(2)}) collective-permute-start(f32[2,64,4096]{2,1,0:T(8,128)S(1)} %add.5383), channel_id=1, source_target_pairs={{0,2},{1,3},{2,0},{3,1},{4,6},{5,7},{6,4},{7,5},{8,10},{9,11},{10,... | collective-permute-start | bytes 6291464 | tf_op jit(solution)/shard_map/ppermute | solution.py:14
  444.1 48.4 %collective-permute-start.8 = (f32[2,64,4096]{2,1,0:T(8,128)S(1)}, f32[2,64,4096]{2,1,0:T(8,128)S(1)}, u32[]{:S(2)}, u32[]{:S(2)}) collective-permute-start(f32[2,64,4096]{2,1,0:T(8,128)S(1)} %pad_maximum_fusion.1), channel_id=1, source_target_pairs={{0,4},{1,5},{2,6},{3,7},{4,0},{5,1},{6,2},{7,3},{8,12},{9,13},{10,... | collective-permute-start | bytes 6291464 | tf_op jit(solution)/shard_map/ppermute | solution.py:14
  492.5 2.0 copy-start
  494.5 46.5 %collective-permute-start.9 = (f32[2,64,4096]{2,1,0:T(8,128)}, f32[2,64,4096]{2,1,0:T(8,128)}, u32[]{:S(2)}, u32[]{:S(2)}) collective-permute-start(f32[2,64,4096]{2,1,0:T(8,128)} %fusion.457), channel_id=1, source_target_pairs={{0,8},{1,9},{2,10},{3,11},{4,12},{5,13},{6,14},{7,15},{8,0},{9,1},... | collective-permute-start | bytes 6291464 | tf_op jit(solution)/shard_map/ppermute | solution.py:14
  556.6 2.0 copy-start.2
  571.5 1.3 copy-start.3
where the time goes:
time: 580 us; the launch traced here: 573 us
  waiting for transfers between devices  240 us (41%)
  other arithmetic  156 us (27%)
  between operations  72 us (12%)
  blocking collectives  40.3 us (7%)
  local copies, waits for them, and re-layouts  33.8 us (6%)
  matrix products  20.4 us (4%)
  starting transfers between devices  11 us (2%)
    ppermute x10, waiting for transfers between devices, from_partner(): lax.ppermute(array, axis, [(i, i ^ 1 << bit) for i in range(lax.axis_size...  240 us
    sub x14, other arithmetic, rotate(): values[0] * cosine - values[1] * sine_part  116 us
    all_to_all x1, blocking collectives, finish_levels(): lax.all_to_all(blocks.reshape(2, node_count, devices, per_source), ('grp'...  40.3 us
    dot_general x8, matrix products, freq_level(): jnp.einsum('ts,rsn->rtn', table_now, rotate(values, -phase_angle), precis...  16.4 us
  transfers between devices with their start and end apart: 10, of which 7 were waited for; matrix products, arithmetic and copies ran while one was open for 11% of the time, Pallas kernels for 0%

commit v1 on v0

--- a/solution.py
+++ b/solution.py
@@ -241,12 +241,20 @@
     blocks = jnp.take(blocks, inverse, axis=2)
     blocks = blocks.reshape(2, node_count, groups, group_width, 2, 2, 2, 2, rest_rows)
     blocks = jnp.transpose(blocks, (0, 1, 2, 4, 5, 6, 7, 3, 8))
-    pair_state = lax.all_to_all(
-        blocks.reshape(2, node_count, devices, per_source),
-        ("grp", "dev"),
-        split_axis=2,
-        concat_axis=2,
-        tiled=True,
+    pair_state = jnp.concatenate(
+        lax.all_to_all(
+            jnp.stack(
+                jnp.split(
+                    blocks.reshape(2, node_count, devices, per_source),
+                    lax.axis_size(("grp", "dev")),
+                    axis=2,
+                )
+            ),
+            ("grp", "dev"),
+            0,
+            0,
+        ),
+        axis=2,
     ).reshape(2, node_count, per_dev)
     middle_x, middle_y, rest_x, rest_y = post_layout(loc_index, per_source, rest_rows)
     column = jnp.take(inverse, own_group * group_width + rest_x)

time: 580 us -> 581 us (level)
    unnamed x12 -> x141, local copies, waits for them, and re-layouts: 9.48 us -> 13.2 us
  transfers between devices with their start and end apart: 10 -> 10, of which waited for: 7 -> 7; matrix products, arithmetic and copies ran while one was open for 11% -> 10% of each run, Pallas kernels for 0% -> 0%
where the time goes in v1:
time: 581 us; the launch traced here: 574 us
  waiting for transfers between devices  240 us (41%)
  other arithmetic  155 us (27%)
  between operations  72 us (12%)
  blocking collectives  40.2 us (7%)
  local copies, waits for them, and re-layouts  35.3 us (6%)
  matrix products  20.4 us (4%)
  starting transfers between devices  11 us (2%)
    ppermute x10, waiting for transfers between devices, from_partner(): lax.ppermute(array, axis, [(i, i ^ 1 << bit) for i in range(lax.axis_size...  240 us
    sub x14, other arithmetic, rotate(): values[0] * cosine - values[1] * sine_part  116 us
    all_to_all x1, blocking collectives, finish_levels(): lax.all_to_all(jnp.stack(jnp.split(blocks.reshape(2, node_count, devices,...  40.2 us
    dot_general x8, matrix products, freq_level(): jnp.einsum('ts,rsn->rtn', table_now, rotate(values, -phase_angle), precis...  16.4 us
    unnamed x141, local copies, waits for them, and re-layouts  13.2 us
  transfers between devices with their start and end apart: 10, of which 7 were waited for; matrix products, arithmetic and copies ran while one was open for 10% of the time, Pallas kernels for 0%

profile of v1, /device:TPU:0, one launch (start us, length us, event | category | flops | bytes accessed | tf_op | source)
XLA Modules:
  0.0 574.3 jit_solution(2637410982830784652)
XLA Ops:
  82.5 6.3 %multiply_subtract_fusion.13 = (f32[1,64,4096]{2,1,0:T(8,128)S(1)}, f32[1,64,4096]{2,1,0:T(8,128)S(1)}) fusion(f32[2,64,4096]{2,1,0:T(8,128)} %param.3, f32[4096]{0:T(1024)S(1)} %get-tuple-element.154, f32[]{:T(128)S(6)} %mul.7297, f32[]{:T(128)S(6)} %mul.7291, f32[4096]{0:T(1024)S(1)} %fusion.362, f32[64]{0:T(128)S(1)} %get-tuple-element.115, ...), kind=kLoop, calls=%fused_computation.399 | loop fusion | flops 8126464 | bytes 4276752 | tf_op jit(solution)/shard_map/sub | solution.py:102
  91.3 5.1 multiply_subtract_fusion.12
  98.5 6.8 %multiply_subtract_fusion.11 = (f32[1,64,4096]{2,1,0:T(8,128)S(1)}, f32[1,64,4096]{2,1,0:T(8,128)S(1)}) fusion(f32[2,64,4096]{2,1,0:T(8,128)} %collective-permute-done.1, f32[4096]{0:T(1024)S(1)} %get-tuple-element.154, f32[]{:T(128)S(6)} %mul.7297, f32[]{:T(128)S(6)} %mul.7291, f32[4096]{0:T(1024)S(1)} %fusion.362, f32[64]{0:T(128)S(1)} %get-tuple-element.115, ...), kind=kLoop, calls=%fused_computation.395 | loop fusion | flops 8126464 | bytes 4276752 | tf_op jit(solution)/shard_map/sub | solution.py:102
  107.4 31.6 %collective-permute-done.2 = f32[2,64,4096]{2,1,0:T(8,128)S(1)} collective-permute-done((f32[2,64,4096]{2,1,0:T(8,128)S(1)}, f32[2,64,4096]{2,1,0:T(8,128)S(1)}, u32[]{:S(2)}, u32[]{:S(2)}) %collective-permute-start.2) | collective-permute-done | bytes 2097184 | tf_op jit(solution)/shard_map/ppermute | solution.py:14
  139.0 5.1 multiply_subtract_fusion.10
  146.1 10.1 %multiply_subtract_fusion.8 = (f32[1,64,4096]{2,1,0:T(8,128)S(1)}, f32[1,64,4096]{2,1,0:T(8,128)S(1)}, f32[1,64,4096]{2,1,0:T(8,128)S(1)}) fusion(f32[4096]{0:T(1024)S(1)} %get-tuple-element.195, f32[]{:T(128)S(6)} %mul.7617, f32[]{:T(128)S(6)} %mul.7611, f32[4096]{0:T(1024)S(1)} %get-tuple-element.194, f32[64]{0:T(128)S(1)} %get-tuple-element.114, ...), kind=kLoop, calls=%fused_computation.389 | loop fusion | flops 15204352 | bytes 5374496 | tf_op jit(solution)/shard_map/sub | solution.py:102
  163.1 43.7 %collective-permute-done.3 = f32[2,64,4096]{2,1,0:T(8,128)} collective-permute-done((f32[2,64,4096]{2,1,0:T(8,128)}, f32[2,64,4096]{2,1,0:T(8,128)}, u32[]{:S(2)}, u32[]{:S(2)}) %collective-permute-start.3) | collective-permute-done | bytes 2097184 | tf_op jit(solution)/shard_map/ppermute | solution.py:14
  208.3 6.3 %multiply_subtract_fusion.7 = (f32[1,64,4096]{2,1,0:T(8,128)S(1)}, f32[1,64,4096]{2,1,0:T(8,128)S(1)}) fusion(f32[2,64,4096]{2,1,0:T(8,128)} %collective-permute-done.3, f32[4096]{0:T(1024)S(1)} %get-tuple-element.195, f32[]{:T(128)S(6)} %mul.7617, f32[]{:T(128)S(6)} %mul.7611, f32[4096]{0:T(1024)S(1)} %get-tuple-element.194, f32[64]{0:T(128)S(1)} %get-tuple-element.114, ...), kind=kLoop, calls=%fused_computation.387 | loop fusion | flops 8126464 | bytes 4276752 | tf_op jit(solution)/shard_map/sub | solution.py:102
  214.6 6.3 %multiply_subtract_fusion.6 = (f32[1,64,4096]{2,1,0:T(8,128)S(1)}, f32[1,64,4096]{2,1,0:T(8,128)S(1)}) fusion(f32[2,64,4096]{2,1,0:T(8,128)} %collective-permute-done.4, f32[4096]{0:T(1024)S(1)} %get-tuple-element.195, f32[]{:T(128)S(6)} %mul.7617, f32[]{:T(128)S(6)} %mul.7611, f32[4096]{0:T(1024)S(1)} %get-tuple-element.194, f32[64]{0:T(128)S(1)} %get-tuple-element.114, ...), kind=kLoop, calls=%fused_computation.385 | loop fusion | flops 8126464 | bytes 4276752 | tf_op jit(solution)/shard_map/sub | solution.py:102
  221.0 32.4 %collective-permute-done.5 = f32[2,64,4096]{2,1,0:T(8,128)} collective-permute-done((f32[2,64,4096]{2,1,0:T(8,128)}, f32[2,64,4096]{2,1,0:T(8,128)}, u32[]{:S(2)}, u32[]{:S(2)}) %collective-permute-start.5) | collective-permute-done | bytes 2097184 | tf_op jit(solution)/shard_map/ppermute | solution.py:14
  253.4 11.4 %multiply_subtract_fusion.5 = (f32[1,64,4096]{2,1,0:T(8,128)S(1)}, f32[1,64,4096]{2,1,0:T(8,128)S(1)}, f32[1,64,4096]{2,1,0:T(8,128)S(1)}) fusion(f32[2,64,4096]{2,1,0:T(8,128)} %collective-permute-done.5, f32[4096]{0:T(1024)S(1)} %get-tuple-element.195, f32[]{:T(128)S(6)} %mul.7617, f32[]{:T(128)S(6)} %mul.7611, f32[4096]{0:T(1024)S(1)} %get-tuple-element.194, ...), kind=kLoop, calls=%fused_computation.383 | loop fusion | flops 15466496 | bytes 7455248 | tf_op jit(solution)/shard_map/sub | solution.py:102
  273.0 6.4 %multiply_subtract_fusion.4 = (f32[1,64,4096]{2,1,0:T(8,128)}, f32[1,64,4096]{2,1,0:T(8,128)S(1)}) fusion(f32[2,64,4096]{2,1,0:T(8,128)S(1)} %fusion, f32[4096]{0:T(1024)S(1)} %get-tuple-element.195, f32[]{:T(128)S(6)} %mul.7617, f32[]{:T(128)S(6)} %mul.7611, f32[64]{0:T(128)S(1)} %get-tuple-element.116, f32[4096]{0:T(1024)S(1)} %get-tuple-element.194, ...), kind=kLoop, calls=%fused_computation.381 | loop fusion | flops 7864320 | bytes 4243984 | tf_op jit(solution)/shard_map/sub | solution.py:102
  288.4 5.0 gather_fusion
  299.9 4.6 reshape.12153
  304.5 40.2 %all_to_all.5 = f32[128,1,4096]{2,1,0:T(1,128)} all-to-all(f32[128,1,4096]{2,1,0:T(1,128)S(1)} %reshape.12153), channel_id=1, replica_groups=mesh['grp'=2,'dev'=64] {'grp','dev'}, dimensions={0} | all-to-all | bytes 4194304 | tf_op jit(solution)/shard_map/all_to_all | solution.py:245
  345.3 7.3 %reduce.18 = f32[128,4096]{1,0:T(8,128)S(1)} reduce(f32[128,1,4096]{2,1,0:T(1,128)} %all_to_all.5, f32[]{:T(128)} %broadcast.18834), dimensions={1}, to_apply=%all_to_all.3.reduce_sub_computation | reduce | bytes 4194308 | tf_op jit(solution)/shard_map/all_to_all | solution.py:245
  375.5 5.6 multiply_add_fusion.16
  381.5 34.5 %collective-permute-done.7 = f32[2,64,4096]{2,1,0:T(8,128)S(1)} collective-permute-done((f32[2,64,4096]{2,1,0:T(8,128)S(1)}, f32[2,64,4096]{2,1,0:T(8,128)S(1)}, u32[]{:S(2)}, u32[]{:S(2)}) %collective-permute-start.7) | collective-permute-done | bytes 2097184 | tf_op jit(solution)/shard_map/ppermute | solution.py:14
  416.3 13.1 %multiply_subtract_fusion.3 = (f32[1,64,4096]{2,1,0:T(8,128)S(1)}, f32[1,64,4096]{2,1,0:T(8,128)S(1)}) fusion(f32[2,64,4096]{2,1,0:T(8,128)S(1)} %add.5384, f32[4096]{0:T(1024)S(1)} %get-tuple-element.13, f32[4096]{0:T(1024)S(1)} %get-tuple-element.203, f32[4096]{0:T(1024)S(1)} %get-tuple-element.204, f32[4096]{0:T(1024)S(1)} %get-tuple-element.158, ...), kind=kLoop, calls=%fused_computation.379 | loop fusion | flops 10747904 | bytes 4309504 | tf_op jit(solution)/shard_map/sub | solution.py:102
  431.4 12.9 %multiply_subtract_fusion.2 = (f32[1,64,4096]{2,1,0:T(8,128)S(1)}, f32[1,64,4096]{2,1,0:T(8,128)S(1)}) fusion(f32[2,64,4096]{2,1,0:T(8,128)S(1)} %convolution_bitcast_fusion.1, f32[4096]{0:T(1024)S(1)} %get-tuple-element.13, f32[4096]{0:T(1024)S(1)} %get-tuple-element.203, f32[4096]{0:T(1024)S(1)} %get-tuple-element.204, f32[4096]{0:T(1024)S(1)} %get-tuple-element.158, ...), kind=kLoop, calls=%fused_computation.377 | loop fusion | flops 10485760 | bytes 4342272 | tf_op jit(solution)/shard_map/sub | solution.py:102
  445.2 47.6 %collective-permute-done.8 = f32[2,64,4096]{2,1,0:T(8,128)S(1)} collective-permute-done((f32[2,64,4096]{2,1,0:T(8,128)S(1)}, f32[2,64,4096]{2,1,0:T(8,128)S(1)}, u32[]{:S(2)}, u32[]{:S(2)}) %collective-permute-start.8) | collective-permute-done | bytes 2097184 | tf_op jit(solution)/shard_map/ppermute | solution.py:14
  496.2 46.0 %collective-permute-done.9 = f32[2,64,4096]{2,1,0:T(8,128)} collective-permute-done((f32[2,64,4096]{2,1,0:T(8,128)}, f32[2,64,4096]{2,1,0:T(8,128)}, u32[]{:S(2)}, u32[]{:S(2)}) %collective-permute-start.9) | collective-permute-done | bytes 2097184 | tf_op jit(solution)/shard_map/ppermute | solution.py:14
  544.8 13.1 %multiply_subtract_fusion.1 = (f32[1,64,4096]{2,1,0:T(8,128)S(1)}, f32[1,64,4096]{2,1,0:T(8,128)S(1)}) fusion(f32[2,64,4096]{2,1,0:T(8,128)S(1)} %fusion.460, f32[4096]{0:T(1024)S(1)} %get-tuple-element.87, f32[4096]{0:T(1024)S(1)} %get-tuple-element.152, f32[4096]{0:T(1024)S(1)} %get-tuple-element.153, f32[4096]{0:T(1024)S(1)} %multiply_add_fusion.14, ...), kind=kLoop, calls=%fused_computation.375 | loop fusion | flops 10747904 | bytes 4309504 | tf_op jit(solution)/shard_map/sub | solution.py:102
  559.9 12.9 %multiply_subtract_fusion = (f32[2,64,4096]{2,1,0:T(8,128)S(1)}, f32[2,64,4096]{2,1,0:T(8,128)S(1)}) fusion(f32[2,64,4096]{2,1,0:T(8,128)S(1)} %convolution_bitcast_fusion, f32[4096]{0:T(1024)S(1)} %get-tuple-element.87, f32[4096]{0:T(1024)S(1)} %get-tuple-element.152, ...), kind=kLoop, output_to_operand_aliasing={{0}: (12, {}), {1}: (12, {})}, calls=%fused_computation.373 | loop fusion | flops 10485760 | bytes 4342784 | tf_op jit(solution)/shard_map/sub | solution.py:102
  (262 shorter events, 87.9 us)
Async XLA Ops:
  0.0 90.8 %collective-permute-start = (f32[2,64,4096]{2,1,0:T(8,128)}, f32[2,64,4096]{2,1,0:T(8,128)S(1)}, u32[]{:S(2)}, u32[]{:S(2)}) collective-permute-start(f32[2,64,4096]{2,1,0:T(8,128)} %param.3), channel_id=1, source_target_pairs={{0,1},{1,0},{2,3},{3,2},{4,5},{5,4},{6,7},{7,6},{8,9},{9,8},{10,11... | collective-permute-start | bytes 6291464 | tf_op jit(solution)/shard_map/ppermute | solution.py:14
  0.0 98.4 %collective-permute-start.1 = (f32[2,64,4096]{2,1,0:T(8,128)}, f32[2,64,4096]{2,1,0:T(8,128)}, u32[]{:S(2)}, u32[]{:S(2)}) collective-permute-start(f32[2,64,4096]{2,1,0:T(8,128)} %param.3), channel_id=1, source_target_pairs={{0,2},{1,3},{2,0},{3,1},{4,6},{5,7},{6,4},{7,5},{8,10},{9,11},{10,... | collective-permute-start | bytes 6291464 | tf_op jit(solution)/shard_map/ppermute | solution.py:14
  90.8 48.1 %collective-permute-start.2 = (f32[2,64,4096]{2,1,0:T(8,128)S(1)}, f32[2,64,4096]{2,1,0:T(8,128)S(1)}, u32[]{:S(2)}, u32[]{:S(2)}) collective-permute-start(f32[2,64,4096]{2,1,0:T(8,128)S(1)} %collective-permute-done), channel_id=1, source_target_pairs={{0,2},{1,3},{2,0},{3,1},{4,6},{5,7},{6,4},{7,5},{8,10},{9,11},{10,... | collective-permute-start | bytes 6291464 | tf_op jit(solution)/shard_map/ppermute | solution.py:14
  146.1 16.7 %copy-start.5 = (s32[16]{0:T(128)S(1)}, s32[16]{0:T(128)}, u32[]{:S(2)}) copy-start(s32[16]{0:T(128)} %param.4) | copy-start | bytes 196
  157.7 49.1 %collective-permute-start.3 = (f32[2,64,4096]{2,1,0:T(8,128)}, f32[2,64,4096]{2,1,0:T(8,128)}, u32[]{:S(2)}, u32[]{:S(2)}) collective-permute-start(f32[2,64,4096]{2,1,0:T(8,128)} %pad_maximum_fusion), channel_id=1, source_target_pairs={{0,4},{1,5},{2,6},{3,7},{4,0},{5,1},{6,2},{7,3},{8,12},{9,13},{10,... | collective-permute-start | bytes 6291464 | tf_op jit(solution)/shard_map/ppermute | solution.py:14
  161.3 53.3 %collective-permute-start.4 = (f32[2,64,4096]{2,1,0:T(8,128)}, f32[2,64,4096]{2,1,0:T(8,128)}, u32[]{:S(2)}, u32[]{:S(2)}) collective-permute-start(f32[2,64,4096]{2,1,0:T(8,128)} %pad_maximum_fusion), channel_id=1, source_target_pairs={{0,8},{1,9},{2,10},{3,11},{4,12},{5,13},{6,14},{7,15},{8,0},{9,1},... | collective-permute-start | bytes 6291464 | tf_op jit(solution)/shard_map/ppermute | solution.py:14
  206.8 46.6 %collective-permute-start.5 = (f32[2,64,4096]{2,1,0:T(8,128)}, f32[2,64,4096]{2,1,0:T(8,128)}, u32[]{:S(2)}, u32[]{:S(2)}) collective-permute-start(f32[2,64,4096]{2,1,0:T(8,128)} %collective-permute-done.3), channel_id=1, source_target_pairs={{0,8},{1,9},{2,10},{3,11},{4,12},{5,13},{6,14},{7,15},{8,0},{9,1},... | collective-permute-start | bytes 6291464 | tf_op jit(solution)/shard_map/ppermute | solution.py:14
  284.4 1.6 copy-start.1
  298.0 1.9 copy-start.2
  363.6 4.2 collective-permute-start.6
  368.1 48.0 %collective-permute-start.7 = (f32[2,64,4096]{2,1,0:T(8,128)S(1)}, f32[2,64,4096]{2,1,0:T(8,128)S(1)}, u32[]{:S(2)}, u32[]{:S(2)}) collective-permute-start(f32[2,64,4096]{2,1,0:T(8,128)S(1)} %add.5383), channel_id=1, source_target_pairs={{0,2},{1,3},{2,0},{3,1},{4,6},{5,7},{6,4},{7,5},{8,10},{9,11},{10,... | collective-permute-start | bytes 6291464 | tf_op jit(solution)/shard_map/ppermute | solution.py:14
  444.4 48.4 %collective-permute-start.8 = (f32[2,64,4096]{2,1,0:T(8,128)S(1)}, f32[2,64,4096]{2,1,0:T(8,128)S(1)}, u32[]{:S(2)}, u32[]{:S(2)}) collective-permute-start(f32[2,64,4096]{2,1,0:T(8,128)S(1)} %pad_maximum_fusion.1), channel_id=1, source_target_pairs={{0,4},{1,5},{2,6},{3,7},{4,0},{5,1},{6,2},{7,3},{8,12},{9,13},{10,... | collective-permute-start | bytes 6291464 | tf_op jit(solution)/shard_map/ppermute | solution.py:14
  492.8 1.3 copy-start
  495.8 46.5 %collective-permute-start.9 = (f32[2,64,4096]{2,1,0:T(8,128)}, f32[2,64,4096]{2,1,0:T(8,128)}, u32[]{:S(2)}, u32[]{:S(2)}) collective-permute-start(f32[2,64,4096]{2,1,0:T(8,128)} %fusion.457), channel_id=1, source_target_pairs={{0,8},{1,9},{2,10},{3,11},{4,12},{5,13},{6,14},{7,15},{8,0},{9,1},... | collective-permute-start | bytes 6291464 | tf_op jit(solution)/shard_map/ppermute | solution.py:14
  544.7 15.1 %copy-start.3 = (f32[2,64,4096]{2,1,0:T(8,128)S(1)}, f32[2,64,4096]{2,1,0:T(8,128)}, u32[]{:S(2)}) copy-start(f32[2,64,4096]{2,1,0:T(8,128)} %custom-call.4) | copy-start | bytes 6291460
  572.7 1.3 copy-start.4
